TPU v7x, 32 devices: a whole 2x2x4 slice. The times are simulated.
32 devices in a mesh: lat: 4 (over y, x), lon: 8 (over z, core).
Axes of the slice: x: 2, y: 2, z: 4, core: 2. Of those that a mesh axis runs over, the one named last changes fastest.
Arguments:
- fine_map: bfloat16 [4, 48, 256, 400], P(None, 'lat', 'lon'), may hold values from -26 to 26
- ocean_mask: int32 [4, 48, 256], P(None, 'lat', 'lon'), may hold values from 0 to 1
- out_grad: bfloat16 [4, 48, 256, 400], P(None, 'lat', 'lon'), may hold values from -6 to 6
- encode_depth: bfloat16 [7, 7, 400], replicated, may hold values from -0.875 to 0.875
- encode_gain: bfloat16 [400], replicated, may hold values from 0.099609375 to 1.8984375
- encode_shift: bfloat16 [400], replicated, may hold values from -3 to 3
- encode_up: bfloat16 [400, 1600], P('lat'), may hold values from -0.3125 to 0.3125
- encode_up_bias: bfloat16 [1600], replicated, may hold values from -3 to 3
- encode_down: bfloat16 [1600, 400], P('lat'), may hold values from -0.15625 to 0.15625
- encode_down_bias: bfloat16 [400], replicated, may hold values from -3 to 3
- widen_weight: bfloat16 [400, 800], P('lat'), may hold values from -0.3125 to 0.3125
- widen_bias: bfloat16 [800], replicated, may hold values from -3 to 3
- bottle_depth: bfloat16 [7, 7, 800], replicated, may hold values from -0.875 to 0.875
- bottle_gain: bfloat16 [800], replicated, may hold values from 0.099609375 to 1.8984375
- bottle_shift: bfloat16 [800], replicated, may hold values from -3 to 3
- bottle_up: bfloat16 [800, 3200], P('lat'), may hold values from -0.21875 to 0.21875
- bottle_up_bias: bfloat16 [3200], replicated, may hold values from -3 to 3
- bottle_down: bfloat16 [3200, 800], P('lat'), may hold values from -0.109375 to 0.109375
- bottle_down_bias: bfloat16 [800], replicated, may hold values from -3 to 3
- merge_weight: bfloat16 [1200, 400], P('lat'), may hold values from -0.1875 to 0.1875
- merge_bias: bfloat16 [400], replicated, may hold values from -3 to 3
- decode_depth: bfloat16 [7, 7, 400], replicated, may hold values from -0.875 to 0.875
- decode_gain: bfloat16 [400], replicated, may hold values from 0.099609375 to 1.8984375
- decode_shift: bfloat16 [400], replicated, may hold values from -3 to 3
- decode_up: bfloat16 [400, 1600], P('lat'), may hold values from -0.3125 to 0.3125
- decode_up_bias: bfloat16 [1600], replicated, may hold values from -3 to 3
- decode_down: bfloat16 [1600, 400], P('lat'), may hold values from -0.15625 to 0.15625
- decode_down_bias: bfloat16 [400], replicated, may hold values from -3 to 3
Outputs:
- result: bfloat16 [4, 48, 256, 400], P(None, 'lat', 'lon')
- fine_grad: bfloat16 [4, 48, 256, 400], P(None, 'lat', 'lon')
- encode_depth_grad: float32 [7, 7, 400], replicated
- encode_gain_grad: float32 [400], replicated
- encode_shift_grad: float32 [400], replicated
- encode_up_grad: float32 [400, 1600], replicated
- encode_up_bias_grad: float32 [1600], replicated
- encode_down_grad: float32 [1600, 400], replicated
- encode_down_bias_grad: float32 [400], replicated
- widen_weight_grad: float32 [400, 800], replicated
- widen_bias_grad: float32 [800], replicated
- bottle_depth_grad: float32 [7, 7, 800], replicated
- bottle_gain_grad: float32 [800], replicated
- bottle_shift_grad: float32 [800], replicated
- bottle_up_grad: float32 [800, 3200], replicated
- bottle_up_bias_grad: float32 [3200], replicated
- bottle_down_grad: float32 [3200, 800], replicated
- bottle_down_bias_grad: float32 [800], replicated
- merge_weight_grad: float32 [1200, 400], replicated
- merge_bias_grad: float32 [400], replicated
- decode_depth_grad: float32 [7, 7, 400], replicated
- decode_gain_grad: float32 [400], replicated
- decode_shift_grad: float32 [400], replicated
- decode_up_grad: float32 [400, 1600], replicated
- decode_up_bias_grad: float32 [1600], replicated
- decode_down_grad: float32 [1600, 400], replicated
- decode_down_bias_grad: float32 [400], replicated
All inputs are finite; a program needn't handle non-finite values.
Results may differ from a plain program's by a relative error of at most 0.018.
Values may be sent and summed in bfloat16 or wider, within the bound.
No kernel may reach another device: no remote copies, remote signals or barrier semaphores. Data moves between devices by JAX's collectives and lax.ppermute only.
A program may use at most 320 MiB of HBM per device.

v0:
```python
import math
import jax
import jax.numpy as jnp
from jax import lax
from jax.sharding import PartitionSpec as P

epsilon = 1e-05


def padded(block, sides, width, periodic):
    for axis, dim in sides:
        count = lax.axis_size(axis)
        forward = [(i, i + 1) for i in range(count - 1)]
        if periodic:
            forward.append((count - 1, 0))
        backward = [(target, source) for source, target in forward]
        low = lax.ppermute(
            lax.slice_in_dim(block, block.shape[dim] - width, None, axis=dim), axis, forward
        )
        high = lax.ppermute(lax.slice_in_dim(block, 0, width, axis=dim), axis, backward)
        block = jnp.concatenate([low, block, high], axis=dim)
    return block


def widen_map(source):
    wrapped = padded(source, (("lon", 2),), 3, True)
    return padded(wrapped, (("lat", 1),), 3, False)


def stencil(extended, kernel, height, breadth):
    taps = kernel.astype(jnp.float32)
    summed = jnp.zeros((extended.shape[0], height, breadth, extended.shape[3]), jnp.float32)
    for across in range(7):
        for column in range(7):
            summed = summed + taps[across, column] * extended[
                :, across : across + height, column : column + breadth, :
            ].astype(jnp.float32)
    return summed


def kernel_terms(extended, grad_mixed, height, breadth):
    upstream = grad_mixed.astype(jnp.float32)
    all_rows = []
    for across in range(7):
        row_terms = []
        for column in range(7):
            window = extended[:, across : across + height, column : column + breadth, :].astype(
                jnp.float32
            )
            row_terms.append(jnp.sum(window * upstream, axis=(0, 1, 2)))
        all_rows.append(jnp.stack(row_terms))
    return jnp.stack(all_rows)


def cross_rows(former, latter):
    return lax.dot_general(
        former, latter, (((0,), (0,)), ((), ())), preferred_element_type=jnp.float32
    )


def by_transpose(former, latter):
    return lax.dot_general(
        former, latter, (((1,), (1,)), ((), ())), preferred_element_type=jnp.float32
    )


def exact_gelu(values):
    return jax.nn.gelu(values, approximate=False)


def block_forward(source, params, sea_mask):
    kernel, scale_gain, norm_shift, up_weight, up_bias, down_weight, down_bias = params
    date_count, height, breadth, channels = source.shape
    extended = widen_map(source)
    mixed = stencil(extended, kernel, height, breadth)
    local_sums = (
        jnp.sum(sea_mask * mixed, axis=(0, 1, 2)),
        jnp.sum(sea_mask * mixed * mixed, axis=(0, 1, 2)),
        jnp.sum(sea_mask),
    )
    first_sum, square_sum, ocean_count = lax.psum(
        (local_sums[0], local_sums[1], local_sums[2]), ("lat", "lon")
    )
    mean_value = first_sum / ocean_count
    norm_factor = lax.rsqrt(square_sum / ocean_count - mean_value * mean_value + epsilon)
    unit_norm = (mixed - mean_value) * norm_factor
    normed = (
        (unit_norm * scale_gain.astype(jnp.float32) + norm_shift.astype(jnp.float32))
        .astype(jnp.bfloat16)
        .reshape(-1, channels)
    )
    hidden = jnp.dot(normed, up_weight, preferred_element_type=jnp.float32) + up_bias.astype(
        jnp.float32
    )
    active = exact_gelu(hidden).astype(jnp.bfloat16)
    branch = jnp.dot(active, down_weight, preferred_element_type=jnp.float32) + down_bias.astype(
        jnp.float32
    )
    output = sea_mask * (source.astype(jnp.float32) + branch.reshape(source.shape))
    stored = (extended, unit_norm, norm_factor, ocean_count, normed, hidden, active)
    return (output, stored)


def block_backward(grad_output, params, sea_mask, stored):
    kernel, scale_gain, norm_shift, up_weight, up_bias, down_weight, down_bias = params
    extended, unit_norm, norm_factor, ocean_count, normed, hidden_store, active = stored
    date_count, height, breadth, channels = unit_norm.shape
    grad_branch = (sea_mask * grad_output).astype(jnp.bfloat16).reshape(-1, channels)
    grad_down = cross_rows(active, grad_branch)
    grad_down_bias = jnp.sum(grad_branch.astype(jnp.float32), axis=0)
    grad_active = by_transpose(grad_branch, down_weight)
    unused_value, gelu_back = jax.vjp(exact_gelu, hidden_store)
    grad_hidden = gelu_back(grad_active)[0].astype(jnp.bfloat16)
    grad_up = cross_rows(normed, grad_hidden)
    grad_up_bias = jnp.sum(grad_hidden.astype(jnp.float32), axis=0)
    grad_normed = by_transpose(grad_hidden, up_weight).reshape(unit_norm.shape)
    local_back = (
        jnp.sum(grad_normed, axis=(0, 1, 2)),
        jnp.sum(grad_normed * unit_norm, axis=(0, 1, 2)),
    )
    grad_shift, grad_gain = lax.psum((local_back[0], local_back[1]), ("lat", "lon"))
    gain_float = scale_gain.astype(jnp.float32)
    grad_mixed = norm_factor * (
        gain_float * grad_normed
        - sea_mask / ocean_count * (gain_float * grad_shift + unit_norm * (gain_float * grad_gain))
    )
    grad_mixed = grad_mixed.astype(jnp.bfloat16)
    grad_extended = widen_map(grad_mixed)
    grad_source = sea_mask * grad_output + stencil(
        grad_extended, kernel[::-1, ::-1], height, breadth
    )
    grad_kernel = kernel_terms(extended, grad_mixed, height, breadth)
    return (
        grad_source,
        (grad_kernel, grad_gain, grad_shift, grad_up, grad_up_bias, grad_down, grad_down_bias),
    )


def unpack(vector, extents):
    pieces = []
    offset = 0
    for extent in extents:
        length = math.prod(extent)
        pieces.append(vector[offset : offset + length].reshape(extent))
        offset = offset + length
    return pieces


def shards(
    fine_map,
    ocean_mask,
    out_grad,
    encode_depth,
    encode_gain,
    encode_shift,
    encode_up,
    encode_up_bias,
    encode_down,
    encode_down_bias,
    widen_weight,
    widen_bias,
    bottle_depth,
    bottle_gain,
    bottle_shift,
    bottle_up,
    bottle_up_bias,
    bottle_down,
    bottle_down_bias,
    merge_weight,
    merge_bias,
    decode_depth,
    decode_gain,
    decode_shift,
    decode_up,
    decode_up_bias,
    decode_down,
    decode_down_bias,
):
    (
        encode_up,
        encode_down,
        widen_weight,
        bottle_up,
        bottle_down,
        merge_weight,
        decode_up,
        decode_down,
    ) = (
        lax.all_gather(encode_up, "lat", axis=0, tiled=True),
        lax.all_gather(encode_down, "lat", axis=0, tiled=True),
        lax.all_gather(widen_weight, "lat", axis=0, tiled=True),
        lax.all_gather(bottle_up, "lat", axis=0, tiled=True),
        lax.all_gather(bottle_down, "lat", axis=0, tiled=True),
        lax.all_gather(merge_weight, "lat", axis=0, tiled=True),
        lax.all_gather(decode_up, "lat", axis=0, tiled=True),
        lax.all_gather(decode_down, "lat", axis=0, tiled=True),
    )
    date_count, height, breadth, channels = fine_map.shape
    half_height, half_breadth = (height // 2, breadth // 2)
    wide_channels = widen_weight.shape[1]
    sea_fine = ocean_mask.astype(jnp.float32)[..., None]
    sea_coarse = jnp.max(
        sea_fine.reshape(date_count, half_height, 2, half_breadth, 2, 1), axis=(2, 4)
    )
    encode = (
        encode_depth,
        encode_gain,
        encode_shift,
        encode_up,
        encode_up_bias,
        encode_down,
        encode_down_bias,
    )
    bottle = (
        bottle_depth,
        bottle_gain,
        bottle_shift,
        bottle_up,
        bottle_up_bias,
        bottle_down,
        bottle_down_bias,
    )
    decode = (
        decode_depth,
        decode_gain,
        decode_shift,
        decode_up,
        decode_up_bias,
        decode_down,
        decode_down_bias,
    )
    merge_upper = merge_weight[:wide_channels]
    merge_lower = merge_weight[wide_channels:]
    encode_out, encode_stored = block_forward(fine_map, encode, sea_fine)
    skip_map = encode_out.astype(jnp.bfloat16)
    skip_rows = skip_map.reshape(-1, channels)
    blocks_fine = skip_map.reshape(date_count, half_height, 2, half_breadth, 2, channels).astype(
        jnp.float32
    )
    pooled = (jnp.sum(blocks_fine, axis=(2, 4)) * 0.25).astype(jnp.bfloat16).reshape(-1, channels)
    coarse_in = jnp.dot(
        pooled, widen_weight, preferred_element_type=jnp.float32
    ) + widen_bias.astype(jnp.float32)
    coarse_in = coarse_in.astype(jnp.bfloat16).reshape(
        date_count, half_height, half_breadth, wide_channels
    )
    coarse_out, coarse_stored = block_forward(coarse_in, bottle, sea_coarse)
    coarse_low = coarse_out.astype(jnp.bfloat16).reshape(-1, wide_channels)
    upper_part = jnp.dot(coarse_low, merge_upper, preferred_element_type=jnp.float32)
    upper_part = upper_part.reshape(date_count, half_height, 1, half_breadth, 1, channels)
    lower_part = jnp.dot(skip_rows, merge_lower, preferred_element_type=jnp.float32)
    lower_part = lower_part.reshape(date_count, half_height, 2, half_breadth, 2, channels)
    merged = (lower_part + upper_part).reshape(
        date_count, height, breadth, channels
    ) + merge_bias.astype(jnp.float32)
    decode_in = merged.astype(jnp.bfloat16)
    decode_out, decode_stored = block_forward(decode_in, decode, sea_fine)
    result = decode_out.astype(jnp.bfloat16)
    grad_decode_in, decode_grads = block_backward(
        out_grad.astype(jnp.float32), decode, sea_fine, decode_stored
    )
    grad_merged = grad_decode_in.astype(jnp.bfloat16).reshape(-1, channels)
    coarse_grid = coarse_low.reshape(date_count, half_height, 1, half_breadth, 1, wide_channels)
    upsampled_rows = jnp.broadcast_to(
        coarse_grid, (date_count, half_height, 2, half_breadth, 2, wide_channels)
    ).reshape(-1, wide_channels)
    grad_merge_weight = jnp.concatenate(
        [cross_rows(upsampled_rows, grad_merged), cross_rows(skip_rows, grad_merged)], axis=0
    )
    grad_merge_bias = jnp.sum(grad_merged.astype(jnp.float32), axis=0)
    grad_upsampled = by_transpose(grad_merged, merge_upper)
    grad_coarse = jnp.sum(
        grad_upsampled.reshape(date_count, half_height, 2, half_breadth, 2, wide_channels),
        axis=(2, 4),
    )
    grad_skip_direct = by_transpose(grad_merged, merge_lower)
    grad_coarse_in, bottle_grads = block_backward(grad_coarse, bottle, sea_coarse, coarse_stored)
    grad_wide = grad_coarse_in.astype(jnp.bfloat16).reshape(-1, wide_channels)
    grad_widen_weight = cross_rows(pooled, grad_wide)
    grad_widen_bias = jnp.sum(grad_wide.astype(jnp.float32), axis=0)
    grad_pooled = (
        by_transpose(grad_wide, widen_weight).reshape(
            date_count, half_height, 1, half_breadth, 1, channels
        )
        * 0.25
    )
    grad_skip = (
        grad_skip_direct.reshape(date_count, half_height, 2, half_breadth, 2, channels)
        + grad_pooled
    )
    grad_skip = grad_skip.reshape(date_count, height, breadth, channels)
    grad_fine, encode_grads = block_backward(grad_skip, encode, sea_fine, encode_stored)
    fine_grad = grad_fine.astype(jnp.bfloat16)
    large_parts = [
        encode_grads[3],
        encode_grads[5],
        grad_widen_weight,
        bottle_grads[3],
        bottle_grads[5],
        grad_merge_weight,
        decode_grads[3],
        decode_grads[5],
    ]
    large_extents = [part_grad.shape for part_grad in large_parts]
    large_vector = jnp.concatenate([part_grad.reshape(-1) for part_grad in large_parts])
    share = lax.psum_scatter(large_vector, ("lat", "lon"), scatter_dimension=0, tiled=True)
    large_total = lax.all_gather(
        share.astype(jnp.bfloat16), ("lat", "lon"), axis=0, tiled=True
    ).astype(share.dtype)
    small_parts = [
        encode_grads[0],
        encode_grads[4],
        encode_grads[6],
        grad_widen_bias,
        bottle_grads[0],
        bottle_grads[4],
        bottle_grads[6],
        grad_merge_bias,
        decode_grads[0],
        decode_grads[4],
        decode_grads[6],
    ]
    small_extents = [part_grad.shape for part_grad in small_parts]
    small_vector = jnp.concatenate([part_grad.reshape(-1) for part_grad in small_parts])
    small_total = lax.psum(small_vector, ("lat", "lon"))
    (
        encode_up_sum,
        encode_down_sum,
        widen_w_sum,
        bottle_up_sum,
        bottle_down_sum,
        merge_w_sum,
        decode_up_sum,
        decode_down_sum,
    ) = unpack(large_total, large_extents)
    (
        encode_kernel_sum,
        encode_upb_sum,
        encode_downb_sum,
        widen_b_sum,
        bottle_kernel_sum,
        bottle_upb_sum,
        bottle_downb_sum,
        merge_b_sum,
        decode_kernel_sum,
        decode_upb_sum,
        decode_downb_sum,
    ) = unpack(small_total, small_extents)
    return (
        result,
        fine_grad,
        encode_kernel_sum,
        encode_grads[1],
        encode_grads[2],
        encode_up_sum,
        encode_upb_sum,
        encode_down_sum,
        encode_downb_sum,
        widen_w_sum,
        widen_b_sum,
        bottle_kernel_sum,
        bottle_grads[1],
        bottle_grads[2],
        bottle_up_sum,
        bottle_upb_sum,
        bottle_down_sum,
        bottle_downb_sum,
        merge_w_sum,
        merge_b_sum,
        decode_kernel_sum,
        decode_grads[1],
        decode_grads[2],
        decode_up_sum,
        decode_upb_sum,
        decode_down_sum,
        decode_downb_sum,
    )


def solution(mesh):
    placed = (
        P(None, "lat", "lon", None),
        P(None, "lat", "lon"),
        P(None, "lat", "lon", None),
        P(),
        P(),
        P(),
        P("lat", None),
        P(),
        P("lat", None),
        P(),
        P("lat", None),
        P(),
        P(),
        P(),
        P(),
        P("lat", None),
        P(),
        P("lat", None),
        P(),
        P("lat", None),
        P(),
        P(),
        P(),
        P(),
        P("lat", None),
        P(),
        P("lat", None),
        P(),
    )
    return jax.shard_map(
        shards,
        mesh=mesh,
        in_specs=placed,
        out_specs=(
            P(None, "lat", "lon", None),
            P(None, "lat", "lon", None),
            P(),
            P(),
            P(),
            P(),
            P(),
            P(),
            P(),
            P(),
            P(),
            P(),
            P(),
            P(),
            P(),
            P(),
            P(),
            P(),
            P(),
            P(),
            P(),
            P(),
            P(),
            P(),
            P(),
            P(),
            P(),
        ),
        check_vma=False,
    )
```

profile of v0, /device:TPU:0, one launch (start us, length us, event | category | flops | bytes accessed | tf_op | source)
XLA Modules:
  0.0 2301.6 jit_solution(13207212915180531190)
XLA Ops:
  32.2 21.0 all-gather.1
  53.2 15.3 all-gather.2
  125.6 26.5 %multiply_reduce_fusion.1 = (f32[400]{0:T(512)}, f32[400]{0:T(512)}, f32[4,12,32,400]{3,2,1,0:T(8,128)}) fusion(f32[4,12,32]{2,1,0:T(8,128)S(1)} %copy-done.50, bf16[4,15,38,400]{3,2,1,0:T(8,128)(2,1)S(1)} %get-tuple-element.441, f32[400]{0:T(512)} %bitcast.523, f32[400]{0:T(512)} %bitcast.522, f32[400]{0:T(512)} %bitcast.521, f32[400]{0:T(512)} %bitcast.520, ...), kind=kLoop, calls=%fused_computation.214 | loop fusion | flops 97688800 | bytes 59185344 | tf_op jit(solution)/shard_map/reduce_sum | solution.py:77
  152.1 43.1 %all-reduce.7 = (f32[400]{0:T(512)S(1)}, f32[]{:T(128)}, f32[400]{0:T(512)S(1)}) all-reduce(f32[400]{0:T(512)} %get-tuple-element.207, f32[]{:T(128)} %convert_reduce_fusion.9, f32[400]{0:T(512)} %get-tuple-element.206), channel_id=1, replica_groups=mesh['lat'=4,'lon'=8] {'lat','lon'}, use_global_device_ids=true, to_apply=%region_5.0 | all-reduce | flops 801 | bytes 6408 | tf_op jit(solution)/shard_map/psum | solution.py:81
  201.4 29.4 %multiply_convert_fusion.1 = (bf16[1536,1600]{0,1:T(8,128)(2,1)}, f32[1536,1600]{0,1:T(8,128)}, f32[1536,1600]{0,1:T(8,128)}) fusion(f32[1600]{0:T(1024)S(1)} %copy-done.321, bf16[1536,400]{1,0:T(8,128)(2,1)S(1)} %bitcast.461, bf16[400,1600]{1,0:T(8,128)(2,1)} %reshape.643), kind=kOutput, calls=%fused_computation.171 | convolution fusion | flops 2128281600 | bytes 27091200 | tf_op jit(solution)/shard_map/dot_general | solution.py:92
  230.8 6.8 convolution_add_fusion.4
  241.2 5.1 convert_reduce_fusion.3
  269.2 12.5 collective-permute-done.6
  281.7 18.0 collective-permute-done.7
  301.5 11.4 multiply_reduce_fusion.4
  313.0 39.1 %all-reduce.6 = (f32[800]{0:T(1024)S(1)}, f32[]{:T(128)}, f32[800]{0:T(1024)S(1)}) all-reduce(f32[800]{0:T(1024)S(1)} %get-tuple-element.279, f32[]{:T(128)} %reduce_sum.1550, f32[800]{0:T(1024)S(1)} %get-tuple-element.278), channel_id=1, replica_groups=mesh['lat'=4,'lon'=8] {'lat','lon'}, use_global_device_ids=true, to_apply=%region_13.0 | all-reduce | flops 1601 | bytes 12808 | tf_op jit(solution)/shard_map/psum | solution.py:81
  353.1 16.4 multiply_convert_fusion.2
  369.6 7.7 multiply_convert_fusion.10
  407.7 12.8 collective-permute-done.11
  425.0 24.8 %multiply_reduce_fusion = (f32[400]{0:T(512)S(1)}, f32[400]{0:T(512)S(1)}, f32[4,12,32,400]{3,2,1,0:T(8,128)}) fusion(f32[4,12,32]{2,1,0:T(8,128)S(1)} %copy-done.52, bf16[4,15,38,400]{3,2,1,0:T(8,128)(2,1)S(1)} %get-tuple-element.437, f32[400]{0:T(512)} %bitcast.594, f32[400]{0:T(512)} %bitcast.593, f32[400]{0:T(512)} %bitcast.592, f32[400]{0:T(512)} %bitcast.591, ...), kind=kLoop, calls=%fused_computation.212 | loop fusion | flops 103218400 | bytes 55614144 | tf_op jit(solution)/shard_map/reduce_sum | solution.py:77
  449.9 38.6 %all-reduce.5 = (f32[400]{0:T(512)S(1)}, f32[400]{0:T(512)S(1)}) all-reduce(f32[400]{0:T(512)S(1)} %get-tuple-element.205, f32[400]{0:T(512)S(1)} %get-tuple-element.204), channel_id=1, replica_groups=mesh['lat'=4,'lon'=8] {'lat','lon'}, use_global_device_ids=true, to_apply=%region_17.0 | all-reduce | flops 800 | bytes 6400 | tf_op jit(solution)/shard_map/psum | solution.py:81
  492.8 30.1 %multiply_convert_fusion = (bf16[1536,1600]{0,1:T(8,128)(2,1)}, f32[1536,1600]{0,1:T(8,128)}, f32[1536,1600]{0,1:T(8,128)}) fusion(f32[1600]{0:T(1024)S(1)} %copy-done.320, bf16[1536,400]{1,0:T(8,128)(2,1)S(1)} %bitcast.463, bf16[400,1600]{1,0:T(8,128)(2,1)S(1)} %copy-done.62), kind=kOutput, calls=%fused_computation.158 | convolution fusion | flops 2128281600 | bytes 27091200 | tf_op jit(solution)/shard_map/dot_general | solution.py:92
  522.9 12.3 convert_reduce_fusion
  539.1 4.7 fusion.471
  550.6 41.1 %all-reduce.4 = (f32[400]{0:T(512)S(1)}, f32[400]{0:T(512)S(1)}) all-reduce(f32[400]{0:T(512)S(1)} %multiply_reduce_fusion.3, f32[400]{0:T(512)S(1)} %get-tuple-element.689), channel_id=1, replica_groups=mesh['lat'=4,'lon'=8] {'lat','lon'}, use_global_device_ids=true, to_apply=%region_21.0 | all-reduce | flops 800 | bytes 6400 | tf_op jit(solution)/shard_map/psum | solution.py:121
  591.7 23.0 %fusion.193 = (f32[400]{0:T(512)S(1)}, f32[400]{0:T(512)S(1)}, f32[400]{0:T(512)S(1)}, f32[400]{0:T(512)S(1)}, f32[400]{0:T(512)S(1)}, /*index=5*/f32[400]{0:T(5...) fusion(bf16[4,15,38,400]{3,2,1,0:T(8,128)(2,1)} %copy-done.4, ...), kind=kLoop, calls=%fused_computation.486 | loop fusion | flops 39314400 | bytes 28305344 | tf_op jit(solution)/shard_map/reduce_sum | solution.py:50
  615.8 9.4 fusion.165
  634.5 5.0 fusion.472
  643.7 6.8 convolution_add_fusion.3
  654.7 13.3 fusion.192
  681.9 12.6 collective-permute-done.15
  698.5 25.1 %convert_reduce_fusion.4 = (f32[400]{0:T(512)}, bf16[4,12,32,400]{3,2,1,0:T(8,128)(2,1)S(1)}) fusion(bf16[4,15,38,400]{3,2,1,0:T(8,128)(2,1)S(1)} %get-tuple-element.433, f32[400]{0:T(512)S(1)} %bitcast.605, f32[400]{0:T(512)S(1)} %bitcast.604, f32[400]{0:T(512)S(1)} %bitcast.603, f32[400]{0:T(512)S(1)} %bitcast.602, f32[400]{0:T(512)S(1)} %bitcast.601, ...), kind=kLoop, calls=%fused_computation.567 | loop fusion | flops 104447600 | bytes 55612544 | tf_op jit(solution)/shard_map/reduce_sum | solution.py:270
  730.9 8.5 fusion.429
  739.5 9.3 convert_reduce_fusion.2
  748.8 7.0 fusion.469
  764.3 39.1 %all-reduce.3 = (f32[800]{0:T(1024)S(1)}, f32[800]{0:T(1024)S(1)}) all-reduce(f32[800]{0:T(1024)S(1)} %multiply_reduce_fusion.5, f32[800]{0:T(1024)S(1)} %get-tuple-element.691), channel_id=1, replica_groups=mesh['lat'=4,'lon'=8] {'lat','lon'}, use_global_device_ids=true, to_apply=%region_26.0 | all-reduce | flops 1600 | bytes 12800 | tf_op jit(solution)/shard_map/psum | solution.py:121
  804.0 5.5 fusion.413
  821.3 6.8 reshape.633
  852.6 11.2 reshape.630
  863.8 14.2 reshape.631
  881.7 11.6 convert_reduce_fusion.8
  906.2 5.8 fusion.431
  912.0 10.7 convert_reduce_fusion.1
  922.8 4.6 fusion.468
  945.3 11.9 dynamic-update-slice.3
  957.2 87.2 %dynamic-update-slice.4 = f32[8480000]{0:T(1024)} dynamic-update-slice(f32[8480000]{0:T(1024)} %dynamic-update-slice.3, f32[2560000]{0:T(1024)} %reshape.630, s32[]{} %constant.210) | dynamic-update-slice | bytes 20480004
  1044.4 87.0 %dynamic-update-slice.5 = f32[8480000]{0:T(1024)} dynamic-update-slice(f32[8480000]{0:T(1024)} %dynamic-update-slice.4, f32[2560000]{0:T(1024)} %reshape.631, s32[]{} %constant.211) | dynamic-update-slice | bytes 20480004
  1131.4 17.6 dynamic-update-slice.6
  1149.0 21.8 dynamic-update-slice.7
  1170.7 22.7 dynamic-update-slice.8
  1199.4 553.5 %all-reduce.15 = (bf16[8480000]{0:T(1024)(128)(2,1)}, f32[400]{0:T(512)S(1)}, f32[400]{0:T(512)S(1)}) all-reduce(f32[8480000]{0:T(1024)} %dynamic-update-slice.8, f32[400]{0:T(512)S(1)} %multiply_reduce_fusion.2, f32[400]{0:T(512)S(1)} %get-tuple-element.693), channel_id=2, replica_groups=mesh['lat'=4,'lon'=8] {'lat','lon'}, use_global_device_ids=true, to_apply=%region_187.0.clone | all-reduce | flops 8480800 | bytes 50886400
  1753.0 10.9 fusion.267
  1764.0 8.8 fusion.239
  1772.9 8.4 fusion.266
  1781.8 8.8 concatenate.399
  1792.1 5.9 broadcast.300
  1798.0 9.0 dynamic-update-slice
  1812.3 5.6 copy.169
  1818.4 4.4 collective-permute-start.22
  1824.1 94.5 %all-reduce.12.cloned.1.call-done = f32[87600]{0:T(1024)} async-done(((f32[87600]{0:T(1024)}), f32[87600]{0:T(1024)}) %all-reduce.12.cloned.1.call-update) | async-done | bytes 350416 | tf_op jit(solution)/shard_map/psum | solution.py:325
  1932.7 25.4 %fusion.269 = bf16[4,12,32,400]{3,2,1,0:T(8,128)(2,1)} fusion(f32[4,12,32,400]{3,0,2,1:T(4,128)S(1)} %bitcast.451, bf16[4,12,32,400]{3,2,1,0:T(8,128)(2,1)S(1)} %copy-done.17, bf16[4,12,3,400]{3,2,1,0:T(4,128)(2,1)S(1)} %collective-permute-done.21, bf16[4,12,3,400]{3,2,1,0:T(4,128)(2,1)S(1)} %collective-permute-done.20, ...), kind=kLoop, calls=%fused_computation.563 | loop fusion | flops 102604800 | bytes 56839744 | tf_op jit(solution)/shard_map/convert_element_type | solution.py:293
  1958.1 249.6 %all-reduce.14.cloned.1.call-done = bf16[8480000]{0:T(1024)(128)(2,1)} async-done(((bf16[8480000]{0:T(1024)(128)(2,1)}), bf16[8480000]{0:T(1024)(128)(2,1)}) %all-reduce.14.cloned.1.call-update) | async-done | bytes 16960016
  2207.7 10.8 fusion.440
  2218.5 13.5 slice.3016
  2232.0 12.2 copy.181
  2244.1 11.7 slice.3013
  2255.8 6.6 fusion.439
  2262.5 4.5 slice.3006
  2269.7 4.6 slice.3026
  (997 shorter events, 338.2 us)
Async XLA Ops:
  7.2 191.1 %all-gather.19.cloned.1.call-start = ((), (), s32[]{:S(2)}) async-start(), calls=%async_computation.6 | async-start | bytes 1730560 | tf_op jit(solution)/shard_map/all_gather | solution.py:189
  8.0 222.9 %all-gather.11.cloned.1.call-start = ((), (), s32[]{:S(2)}) async-start(), calls=%async_computation | async-start | bytes 2048000 | tf_op jit(solution)/shard_map/all_gather | solution.py:190
  8.7 344.4 %all-gather.13.cloned.1.call-start = ((), (), s32[]{:S(2)}) async-start(), calls=%async_computation.1 | async-start | bytes 6400000 | tf_op jit(solution)/shard_map/all_gather | solution.py:192
  9.4 360.1 %all-gather.15.cloned.1.call-start = ((), (), s32[]{:S(2)}) async-start(), calls=%async_computation.2 | async-start | bytes 7168000 | tf_op jit(solution)/shard_map/all_gather | solution.py:193
  10.0 388.8 %all-gather.21.cloned.1.call-start = ((), (), s32[]{:S(2)}) async-start(), calls=%async_computation.7 | async-start | bytes 1730560 | tf_op jit(solution)/shard_map/all_gather | solution.py:195
  10.6 512.3 %all-gather.17.cloned.1.call-start = ((), (), s32[]{:S(2)}) async-start(), calls=%async_computation.3 | async-start | bytes 2048000 | tf_op jit(solution)/shard_map/all_gather | solution.py:196
  11.6 57.0 %collective-permute-start = (bf16[4,12,3,400]{3,2,1,0:T(4,128)(2,1)}, bf16[4,12,3,400]{3,2,1,0:T(4,128)(2,1)}, u32[]{:S(2)}, u32[]{:S(2)}) collective-permute-start(bf16[4,12,3,400]{3,2,1,0:T(4,128)(2,1)} %get-tuple-element.451), channel_id=1, source_target_pairs={{0,1},{1,2},{2,3},{3,4},{4,5},{5,6},{6,7},{7,0},{8,9},{9,10},{10,1... | collective-permute-start | bytes 345608 | tf_op jit(solution)/shard_map/ppermute | solution.py:17
  12.0 56.6 %collective-permute-start.1 = (bf16[4,12,3,400]{3,2,1,0:T(4,128)(2,1)}, bf16[4,12,3,400]{3,2,1,0:T(4,128)(2,1)}, u32[]{:S(2)}, u32[]{:S(2)}) collective-permute-start(bf16[4,12,3,400]{3,2,1,0:T(4,128)(2,1)} %get-tuple-element.452), channel_id=1, source_target_pairs={{1,0},{2,1},{3,2},{4,3},{5,4},{6,5},{7,6},{0,7},{9,8},{10,9},{11,1... | collective-permute-start | bytes 345608 | tf_op jit(solution)/shard_map/ppermute | solution.py:20
  16.1 1902.5 %all-reduce.12.cloned.1.call-start = ((), (), s32[]{:S(2)}) async-start(), calls=%async_computation.4 | async-start | bytes 704512 | tf_op jit(solution)/shard_map/psum | solution.py:325
  29.7 45.9 %copy-start.84 = (s32[4,12,32]{2,0,1:T(4,128)S(1)}, s32[4,12,32]{2,0,1:T(4,128)}, u32[]{:S(2)}) copy-start(s32[4,12,32]{2,0,1:T(4,128)} %param.29) | copy-start | bytes 18436
  70.9 50.0 %collective-permute-start.2 = (bf16[4,3,38,400]{3,2,1,0:T(8,128)(2,1)}, bf16[4,3,38,400]{3,2,1,0:T(8,128)(2,1)}, u32[]{:S(2)}, u32[]{:S(2)}) collective-permute-start(bf16[4,3,38,400]{3,2,1,0:T(8,128)(2,1)} %get-tuple-element.442), channel_id=1, source_target_pairs={{0,8},{8,16},{16,24},{1,9},{9,17},{17,25},{2,10},{10,18},{18,26},{... | collective-permute-start | bytes 1094408 | tf_op jit(solution)/shard_map/ppermute | solution.py:17
  73.8 47.1 %collective-permute-start.3 = (bf16[4,3,38,400]{3,2,1,0:T(8,128)(2,1)}, bf16[4,3,38,400]{3,2,1,0:T(8,128)(2,1)}, u32[]{:S(2)}, u32[]{:S(2)}) collective-permute-start(bf16[4,3,38,400]{3,2,1,0:T(8,128)(2,1)} %get-tuple-element.443), channel_id=1, source_target_pairs={{8,0},{16,8},{24,16},{9,1},{17,9},{25,17},{10,2},{18,10},{26,18},{... | collective-permute-start | bytes 1094408 | tf_op jit(solution)/shard_map/ppermute | solution.py:20
  96.9 204.1 %copy-start.73 = (f32[4,6,16]{2,1,0:T(8,128)}, f32[4,6,16]{2,1,0:T(8,128)S(1)}, u32[]{:S(2)}) copy-start(f32[4,6,16]{2,1,0:T(8,128)S(1)} %copy.154) | copy-start | bytes 4612
  253.7 47.4 %copy-start.23 = (bf16[384,800]{1,0:T(8,128)(2,1)}, bf16[384,800]{1,0:T(8,128)(2,1)S(1)}, u32[]{:S(2)}) copy-start(bf16[384,800]{1,0:T(8,128)(2,1)S(1)} %copy.155) | copy-start | bytes 1843204
  253.8 7.9 collective-permute-start.4
  253.9 7.8 collective-permute-start.5
  261.7 39.4 %copy-start.46 = (bf16[4,6,3,800]{3,2,1,0:T(4,128)(2,1)}, bf16[4,6,3,800]{3,2,1,0:T(4,128)(2,1)S(1)}, u32[]{:S(2)}) copy-start(bf16[4,6,3,800]{3,2,1,0:T(4,128)(2,1)S(1)} %collective-permute-done.4) | copy-start | bytes 345604
  261.7 39.4 %copy-start.48 = (bf16[4,6,3,800]{3,2,1,0:T(4,128)(2,1)}, bf16[4,6,3,800]{3,2,1,0:T(4,128)(2,1)S(1)}, u32[]{:S(2)}) copy-start(bf16[4,6,3,800]{3,2,1,0:T(4,128)(2,1)S(1)} %collective-permute-done.5) | copy-start | bytes 345604
  262.4 38.7 %copy-start.101 = (f32[800]{0:T(1024)S(1)}, f32[800]{0:T(1024)}, u32[]{:S(2)}) copy-start(f32[800]{0:T(1024)} %get-tuple-element.340) | copy-start | bytes 9604
  262.4 38.7 %copy-start.102 = (f32[800]{0:T(1024)S(1)}, f32[800]{0:T(1024)}, u32[]{:S(2)}) copy-start(f32[800]{0:T(1024)} %get-tuple-element.341) | copy-start | bytes 9604
  262.4 38.7 %copy-start.103 = (f32[800]{0:T(1024)S(1)}, f32[800]{0:T(1024)}, u32[]{:S(2)}) copy-start(f32[800]{0:T(1024)} %get-tuple-element.342) | copy-start | bytes 9604
  262.4 38.7 %copy-start.104 = (f32[800]{0:T(1024)S(1)}, f32[800]{0:T(1024)}, u32[]{:S(2)}) copy-start(f32[800]{0:T(1024)} %get-tuple-element.343) | copy-start | bytes 9604
  262.5 38.7 %copy-start.105 = (f32[800]{0:T(1024)S(1)}, f32[800]{0:T(1024)}, u32[]{:S(2)}) copy-start(f32[800]{0:T(1024)} %get-tuple-element.344) | copy-start | bytes 9604
  262.5 38.7 %copy-start.106 = (f32[800]{0:T(1024)S(1)}, f32[800]{0:T(1024)}, u32[]{:S(2)}) copy-start(f32[800]{0:T(1024)} %get-tuple-element.345) | copy-start | bytes 9604
  262.5 38.7 %copy-start.107 = (f32[800]{0:T(1024)S(1)}, f32[800]{0:T(1024)}, u32[]{:S(2)}) copy-start(f32[800]{0:T(1024)} %get-tuple-element.346) | copy-start | bytes 9604
  262.5 38.7 %copy-start.108 = (f32[800]{0:T(1024)S(1)}, f32[800]{0:T(1024)}, u32[]{:S(2)}) copy-start(f32[800]{0:T(1024)} %get-tuple-element.347) | copy-start | bytes 9604
  262.5 38.7 %copy-start.109 = (f32[800]{0:T(1024)S(1)}, f32[800]{0:T(1024)}, u32[]{:S(2)}) copy-start(f32[800]{0:T(1024)} %get-tuple-element.348) | copy-start | bytes 9604
  262.5 38.7 %copy-start.110 = (f32[800]{0:T(1024)S(1)}, f32[800]{0:T(1024)}, u32[]{:S(2)}) copy-start(f32[800]{0:T(1024)} %get-tuple-element.349) | copy-start | bytes 9604
  262.5 38.7 %copy-start.111 = (f32[800]{0:T(1024)S(1)}, f32[800]{0:T(1024)}, u32[]{:S(2)}) copy-start(f32[800]{0:T(1024)} %get-tuple-element.350) | copy-start | bytes 9604
  262.5 38.7 %copy-start.112 = (f32[800]{0:T(1024)S(1)}, f32[800]{0:T(1024)}, u32[]{:S(2)}) copy-start(f32[800]{0:T(1024)} %get-tuple-element.351) | copy-start | bytes 9604
  262.8 18.9 collective-permute-start.6
  266.6 33.1 %collective-permute-start.7 = (bf16[4,3,22,800]{3,2,1,0:T(8,128)(2,1)S(1)}, bf16[4,3,22,800]{3,2,1,0:T(8,128)(2,1)S(1)}, u32[]{:S(2)}, u32[]{:S(2)}) collective-permute-start(bf16[4,3,22,800]{3,2,1,0:T(8,128)(2,1)S(1)} %get-tuple-element.460), channel_id=1, source_target_pairs={{8,0},{16,8},{24,16},{9,1},{17,9},{25,17},{10,2},{18,10},{26,18},{... | collective-permute-start | bytes 1267208 | tf_op jit(solution)/shard_map/ppermute | solution.py:20
  301.5 51.3 %copy-start.93 = (f32[800]{0:T(1024)S(1)}, f32[800]{0:T(1024)}, u32[]{:S(2)}) copy-start(f32[800]{0:T(1024)} %convert_element_type.1354) | copy-start | bytes 9604
  301.5 51.3 %copy-start.139 = (f32[800]{0:T(1024)S(1)}, f32[800]{0:T(1024)}, u32[]{:S(2)}) copy-start(f32[800]{0:T(1024)} %convert_element_type.1355) | copy-start | bytes 9604
  313.0 56.5 %copy-start.21 = (f32[4,6,16,800]{3,2,1,0:T(8,128)}, f32[4,6,16,800]{3,2,1,0:T(8,128)S(1)}, u32[]{:S(2)}) copy-start(f32[4,6,16,800]{3,2,1,0:T(8,128)S(1)} %get-tuple-element.418) | copy-start | bytes 3686404
  383.7 8.3 collective-permute-start.8
  383.8 8.3 collective-permute-start.9
  392.6 15.1 collective-permute-start.10
  396.8 23.6 %collective-permute-start.11 = (bf16[4,3,38,400]{3,2,1,0:T(8,128)(2,1)S(1)}, bf16[4,3,38,400]{3,2,1,0:T(8,128)(2,1)}, u32[]{:S(2)}, u32[]{:S(2)}) collective-permute-start(bf16[4,3,38,400]{3,2,1,0:T(8,128)(2,1)S(1)} %get-tuple-element.439), channel_id=1, source_target_pairs={{8,0},{16,8},{24,16},{9,1},{17,9},{25,17},{10,2},{18,10},{26,18},{... | collective-permute-start | bytes 1094408 | tf_op jit(solution)/shard_map/ppermute | solution.py:20
  398.8 192.9 %copy-start.81 = (f32[4,12,32]{2,1,0:T(8,128)}, f32[4,12,32]{2,1,0:T(8,128)S(1)}, u32[]{:S(2)}) copy-start(f32[4,12,32]{2,1,0:T(8,128)S(1)} %copy.162) | copy-start | bytes 18436
  425.0 64.2 %copy-start.100 = (f32[400]{0:T(512)S(1)}, f32[400]{0:T(512)}, u32[]{:S(2)}) copy-start(f32[400]{0:T(512)} %convert_element_type.1413) | copy-start | bytes 4804
  449.8 42.9 %copy-start.320 = (f32[1600]{0:T(1024)S(1)}, f32[1600]{0:T(1024)}, u32[]{:S(2)}) copy-start(f32[1600]{0:T(1024)} %convert_element_type.1416) | copy-start | bytes 19204
  547.2 44.5 %copy-start.324 = (bf16[400]{0:T(512)(128)(2,1)S(1)}, bf16[400]{0:T(512)(128)(2,1)}, u32[]{:S(2)}) copy-start(bf16[400]{0:T(512)(128)(2,1)} %param.50) | copy-start | bytes 2404
  626.7 41.5 %collective-permute-start.12 = (bf16[4,12,3,400]{3,2,1,0:T(4,128)(2,1)}, bf16[4,12,3,400]{3,2,1,0:T(4,128)(2,1)S(1)}, u32[]{:S(2)}, u32[]{:S(2)}) collective-permute-start(bf16[4,12,3,400]{3,2,1,0:T(4,128)(2,1)} %get-tuple-element.447), channel_id=1, source_target_pairs={{0,1},{1,2},{2,3},{3,4},{4,5},{5,6},{6,7},{7,0},{8,9},{9,10},{10,1... | collective-permute-start | bytes 345608 | tf_op jit(solution)/shard_map/ppermute | solution.py:17
  626.7 41.5 %collective-permute-start.13 = (bf16[4,12,3,400]{3,2,1,0:T(4,128)(2,1)}, bf16[4,12,3,400]{3,2,1,0:T(4,128)(2,1)}, u32[]{:S(2)}, u32[]{:S(2)}) collective-permute-start(bf16[4,12,3,400]{3,2,1,0:T(4,128)(2,1)} %get-tuple-element.448), channel_id=1, source_target_pairs={{1,0},{2,1},{3,2},{4,3},{5,4},{6,5},{7,6},{0,7},{9,8},{10,9},{11,1... | collective-permute-start | bytes 345608 | tf_op jit(solution)/shard_map/ppermute | solution.py:20
  670.1 11.8 collective-permute-start.14
  674.3 20.2 collective-permute-start.15
  759.7 43.7 %copy-start.319 = (bf16[800]{0:T(1024)(128)(2,1)S(1)}, bf16[800]{0:T(1024)(128)(2,1)}, u32[]{:S(2)}) copy-start(bf16[800]{0:T(1024)(128)(2,1)} %param.41) | copy-start | bytes 4804
  759.7 44.3 %copy-start.7 = (bf16[4,9,22,800]{3,2,1,0:T(8,128)(2,1)S(1)}, bf16[4,9,22,800]{3,2,1,0:T(8,128)(2,1)}, u32[]{:S(2)}) copy-start(bf16[4,9,22,800]{3,2,1,0:T(8,128)(2,1)} %copy-done.6) | copy-start | bytes 3801604
  759.7 44.3 %copy-start.87 = (f32[4,6,16]{2,1,0:T(8,128)S(1)}, f32[4,6,16]{2,1,0:T(8,128)}, u32[]{:S(2)}) copy-start(f32[4,6,16]{2,1,0:T(8,128)} %copy.168) | copy-start | bytes 4612
  759.7 44.3 %copy-start.94 = (f32[800]{0:T(1024)S(1)}, f32[800]{0:T(1024)}, u32[]{:S(2)}) copy-start(f32[800]{0:T(1024)} %convert_element_type.1354) | copy-start | bytes 9604
  828.1 9.8 collective-permute-start.16
  828.1 9.8 collective-permute-start.17
  839.5 39.3 %collective-permute-start.18 = (bf16[4,3,22,800]{3,2,1,0:T(8,128)(2,1)}, bf16[4,3,22,800]{3,2,1,0:T(8,128)(2,1)S(1)}, u32[]{:S(2)}, u32[]{:S(2)}) collective-permute-start(bf16[4,3,22,800]{3,2,1,0:T(8,128)(2,1)} %get-tuple-element.455), channel_id=1, source_target_pairs={{0,8},{8,16},{16,24},{1,9},{9,17},{17,25},{2,10},{10,18},{18,26},{... | collective-permute-start | bytes 1267208 | tf_op jit(solution)/shard_map/ppermute | solution.py:17
  843.8 35.1 %collective-permute-start.19 = (bf16[4,3,22,800]{3,2,1,0:T(8,128)(2,1)}, bf16[4,3,22,800]{3,2,1,0:T(8,128)(2,1)}, u32[]{:S(2)}, u32[]{:S(2)}) collective-permute-start(bf16[4,3,22,800]{3,2,1,0:T(8,128)(2,1)} %get-tuple-element.456), channel_id=1, source_target_pairs={{8,0},{16,8},{24,16},{9,1},{17,9},{25,17},{10,2},{18,10},{26,18},{... | collective-permute-start | bytes 1267208 | tf_op jit(solution)/shard_map/ppermute | solution.py:20
  1199.4 553.5 %copy-start.326 = (bf16[400]{0:T(512)(128)(2,1)S(1)}, bf16[400]{0:T(512)(128)(2,1)}, u32[]{:S(2)}) copy-start(bf16[400]{0:T(512)(128)(2,1)} %param.32) | copy-start | bytes 2404
  1199.4 553.6 %copy-start.3 = (bf16[4,15,38,400]{3,2,1,0:T(8,128)(2,1)S(1)}, bf16[4,15,38,400]{3,2,1,0:T(8,128)(2,1)}, u32[]{:S(2)}) copy-start(bf16[4,15,38,400]{3,2,1,0:T(8,128)(2,1)} %copy-done.2) | copy-start | bytes 5472004
  1199.4 553.6 %copy-start.82 = (f32[4,12,32]{2,1,0:T(8,128)S(1)}, f32[4,12,32]{2,1,0:T(8,128)}, u32[]{:S(2)}) copy-start(f32[4,12,32]{2,1,0:T(8,128)} %copy-done.81) | copy-start | bytes 18436
  1199.4 553.6 %copy-start.99 = (f32[400]{0:T(512)S(1)}, f32[400]{0:T(512)}, u32[]{:S(2)}) copy-start(f32[400]{0:T(512)} %convert_element_type.1291) | copy-start | bytes 4804
  1790.6 417.0 %all-reduce.14.cloned.1.call-start = ((), (), s32[]{:S(2)}) async-start(), calls=%async_computation.5 | async-start | bytes 33923072
  1808.6 9.2 collective-permute-start.20
  1808.7 9.2 collective-permute-start.21
  1818.4 110.0 %collective-permute-start.22 = (bf16[4,3,38,400]{3,2,1,0:T(8,128)(2,1)S(1)}, bf16[4,3,38,400]{3,2,1,0:T(8,128)(2,1)}, u32[]{:S(2)}, u32[]{:S(2)}) collective-permute-start(bf16[4,3,38,400]{3,2,1,0:T(8,128)(2,1)S(1)} %get-tuple-element.430), channel_id=1, source_target_pairs={{0,8},{8,16},{16,24},{1,9},{9,17},{17,25},{2,10},{10,18},{18,26},{... | collective-permute-start | bytes 1094408 | tf_op jit(solution)/shard_map/ppermute | solution.py:17
  1822.8 105.6 %collective-permute-start.23 = (bf16[4,3,38,400]{3,2,1,0:T(8,128)(2,1)S(1)}, bf16[4,3,38,400]{3,2,1,0:T(8,128)(2,1)}, u32[]{:S(2)}, u32[]{:S(2)}) collective-permute-start(bf16[4,3,38,400]{3,2,1,0:T(8,128)(2,1)S(1)} %get-tuple-element.431), channel_id=1, source_target_pairs={{8,0},{16,8},{24,16},{9,1},{17,9},{25,17},{10,2},{18,10},{26,18},{... | collective-permute-start | bytes 1094408 | tf_op jit(solution)/shard_map/ppermute | solution.py:20
  (309 other events, 3966.6 us)
Sparse Core Ops, SparseCore 0:
  9.9 34.9 all-gather.18
  46.7 43.4 all-gather.10
  92.1 60.4 all-gather.12
  154.3 66.2 all-gather.14
  222.3 29.3 all-gather.20
  253.4 41.3 all-gather.16
  1790.8 127.8 all-reduce.11
  1926.0 281.6 all-reduce.13
where the time goes:
time: 2330 us; the launch traced here: 2300 us
  blocking collectives  791 us (34%)
  local copies, waits for them, and re-layouts  543 us (23%)
  waiting for transfers between devices  415 us (18%)
  other arithmetic  286 us (12%)
  matrix products  192 us (8%)
  starting transfers between devices  54.6 us (2%)
    unnamed x1, blocking collectives  554 us
    unnamed x720, local copies, waits for them, and re-layouts  288 us
    unnamed x9, waiting for transfers between devices  253 us
    psum x3, blocking collectives, block_forward(): lax.psum((local_sums[0], local_sums[1], local_sums[2]), ('lat', 'lon'))  121 us
    psum x1, waiting for transfers between devices, shards(): small_total = lax.psum(small_vector, ('lat', 'lon'))  94.5 us
    reduce_sum x11, other arithmetic, kernel_terms(): row_terms.append(jnp.sum(window * upstream, axis=(0, 1, 2)))  88.1 us
    psum x2, blocking collectives, block_backward(): lax.psum((local_back[0], local_back[1]), ('lat', 'lon'))  80.2 us
    dot_general x3, matrix products, block_forward(): jnp.dot(normed, up_weight, preferred_element_type=jnp.float32)  76 us
  transfers between devices with their start and end apart: 32, of which 10 were waited for; matrix products, arithmetic and copies ran while one was open for 18% of the time, Pallas kernels for 0%

commit v1 on v0

--- a/solution.py
+++ b/solution.py
@@ -322,7 +322,7 @@
     ]
     small_extents = [part_grad.shape for part_grad in small_parts]
     small_vector = jnp.concatenate([part_grad.reshape(-1) for part_grad in small_parts])
-    small_total = lax.psum(small_vector, ("lat", "lon"))
+    small_total = jnp.sum(lax.all_gather(small_vector, ("lat", "lon")), axis=0)
     (
         encode_up_sum,
         encode_down_sum,

time: 2330 us -> 2420 us (1.039)
  waiting for transfers between devices: 415 us -> 499 us
    unnamed x9 -> x10, waiting for transfers between devices: 253 us -> 392 us
    psum x1 -> x0, waiting for transfers between devices: 94.5 us -> none  [shards(): small_total = lax.psum(small_vector, ('lat', 'lon'))]
    unnamed x720 -> x722, local copies, waits for them, and re-layouts: 288 us -> 298 us
  transfers between devices with their start and end apart: 32 -> 32, of which waited for: 10 -> 13; matrix products, arithmetic and copies ran while one was open for 18% -> 18% of each run, Pallas kernels for 0% -> 0%
where the time goes in v1:
time: 2420 us; the launch traced here: 2400 us
  blocking collectives  792 us (33%)
  local copies, waits for them, and re-layouts  551 us (23%)
  waiting for transfers between devices  499 us (21%)
  other arithmetic  291 us (12%)
  matrix products  192 us (8%)
  starting transfers between devices  52.9 us (2%)
    unnamed x1, blocking collectives  555 us
    unnamed x10, waiting for transfers between devices  392 us
    unnamed x722, local copies, waits for them, and re-layouts  298 us
    psum x3, blocking collectives, block_forward(): lax.psum((local_sums[0], local_sums[1], local_sums[2]), ('lat', 'lon'))  120 us
    reduce_sum x11, other arithmetic, kernel_terms(): row_terms.append(jnp.sum(window * upstream, axis=(0, 1, 2)))  88.2 us
    psum x2, blocking collectives, block_backward(): lax.psum((local_back[0], local_back[1]), ('lat', 'lon'))  80.6 us
    dot_general x3, matrix products, block_forward(): jnp.dot(normed, up_weight, preferred_element_type=jnp.float32)  75.9 us
    slice x18, local copies, waits for them, and re-layouts, unpack(): pieces.append(vector[offset:offset + length].reshape(extent))  70.1 us
  transfers between devices with their start and end apart: 32, of which 13 were waited for; matrix products, arithmetic and copies ran while one was open for 18% of the time, Pallas kernels for 0%

profile of v1, /device:TPU:0, one launch (start us, length us, event | category | flops | bytes accessed | tf_op | source)
XLA Modules:
  0.0 2397.5 jit_solution(13020585841129519735)
XLA Ops:
  32.2 21.0 all-gather.2
  53.2 15.3 all-gather.3
  122.9 26.5 %multiply_reduce_fusion.1 = (f32[400]{0:T(512)}, f32[400]{0:T(512)}, f32[4,12,32,400]{3,2,1,0:T(8,128)}) fusion(f32[4,12,32]{2,1,0:T(8,128)S(1)} %copy-done.50, bf16[4,15,38,400]{3,2,1,0:T(8,128)(2,1)S(1)} %get-tuple-element.468, f32[400]{0:T(512)} %bitcast.523, f32[400]{0:T(512)} %bitcast.522, f32[400]{0:T(512)} %bitcast.521, f32[400]{0:T(512)} %bitcast.520, ...), kind=kLoop, calls=%fused_computation.214 | loop fusion | flops 97688800 | bytes 59185344 | tf_op jit(solution)/shard_map/reduce_sum | solution.py:77
  149.4 42.3 %all-reduce.8 = (f32[400]{0:T(512)S(1)}, f32[]{:T(128)}, f32[400]{0:T(512)S(1)}) all-reduce(f32[400]{0:T(512)} %get-tuple-element.234, f32[]{:T(128)} %convert_reduce_fusion.9, f32[400]{0:T(512)} %get-tuple-element.233), channel_id=1, replica_groups=mesh['lat'=4,'lon'=8] {'lat','lon'}, use_global_device_ids=true, to_apply=%region_5.0 | all-reduce | flops 801 | bytes 6408 | tf_op jit(solution)/shard_map/psum | solution.py:81
  198.0 29.4 %multiply_convert_fusion.1 = (bf16[1536,1600]{0,1:T(8,128)(2,1)}, f32[1536,1600]{0,1:T(8,128)}, f32[1536,1600]{0,1:T(8,128)}) fusion(f32[1600]{0:T(1024)S(1)} %copy-done.321, bf16[1536,400]{1,0:T(8,128)(2,1)S(1)} %bitcast.461, bf16[400,1600]{1,0:T(8,128)(2,1)} %reshape.646), kind=kOutput, calls=%fused_computation.171 | convolution fusion | flops 2128281600 | bytes 27091200 | tf_op jit(solution)/shard_map/dot_general | solution.py:92
  227.4 7.0 convolution_add_fusion.4
  238.0 4.9 convert_reduce_fusion.3
  266.6 10.1 collective-permute-done.6
  276.7 22.0 collective-permute-done.7
  300.5 11.4 multiply_reduce_fusion.4
  312.0 39.7 %all-reduce.7 = (f32[800]{0:T(1024)S(1)}, f32[]{:T(128)}, f32[800]{0:T(1024)S(1)}) all-reduce(f32[800]{0:T(1024)S(1)} %get-tuple-element.306, f32[]{:T(128)} %reduce_sum.1559, f32[800]{0:T(1024)S(1)} %get-tuple-element.305), channel_id=1, replica_groups=mesh['lat'=4,'lon'=8] {'lat','lon'}, use_global_device_ids=true, to_apply=%region_13.0 | all-reduce | flops 1601 | bytes 12808 | tf_op jit(solution)/shard_map/psum | solution.py:81
  352.7 16.4 multiply_convert_fusion.2
  369.2 7.7 multiply_convert_fusion.10
  407.1 12.7 collective-permute-done.11
  424.5 24.8 %multiply_reduce_fusion = (f32[400]{0:T(512)S(1)}, f32[400]{0:T(512)S(1)}, f32[4,12,32,400]{3,2,1,0:T(8,128)}) fusion(f32[4,12,32]{2,1,0:T(8,128)S(1)} %copy-done.52, bf16[4,15,38,400]{3,2,1,0:T(8,128)(2,1)S(1)} %get-tuple-element.464, f32[400]{0:T(512)} %bitcast.594, f32[400]{0:T(512)} %bitcast.593, f32[400]{0:T(512)} %bitcast.592, f32[400]{0:T(512)} %bitcast.591, ...), kind=kLoop, calls=%fused_computation.212 | loop fusion | flops 103218400 | bytes 55614144 | tf_op jit(solution)/shard_map/reduce_sum | solution.py:77
  449.4 38.3 %all-reduce.6 = (f32[400]{0:T(512)S(1)}, f32[400]{0:T(512)S(1)}) all-reduce(f32[400]{0:T(512)S(1)} %get-tuple-element.232, f32[400]{0:T(512)S(1)} %get-tuple-element.231), channel_id=1, replica_groups=mesh['lat'=4,'lon'=8] {'lat','lon'}, use_global_device_ids=true, to_apply=%region_17.0 | all-reduce | flops 800 | bytes 6400 | tf_op jit(solution)/shard_map/psum | solution.py:81
  492.0 30.1 %multiply_convert_fusion = (bf16[1536,1600]{0,1:T(8,128)(2,1)}, f32[1536,1600]{0,1:T(8,128)}, f32[1536,1600]{0,1:T(8,128)}) fusion(f32[1600]{0:T(1024)S(1)} %copy-done.320, bf16[1536,400]{1,0:T(8,128)(2,1)S(1)} %bitcast.463, bf16[400,1600]{1,0:T(8,128)(2,1)S(1)} %copy-done.62), kind=kOutput, calls=%fused_computation.158 | convolution fusion | flops 2128281600 | bytes 27091200 | tf_op jit(solution)/shard_map/dot_general | solution.py:92
  522.2 12.3 convert_reduce_fusion
  538.4 4.7 fusion.471
  549.8 41.5 %all-reduce.5 = (f32[400]{0:T(512)S(1)}, f32[400]{0:T(512)S(1)}) all-reduce(f32[400]{0:T(512)S(1)} %multiply_reduce_fusion.3, f32[400]{0:T(512)S(1)} %get-tuple-element.716), channel_id=1, replica_groups=mesh['lat'=4,'lon'=8] {'lat','lon'}, use_global_device_ids=true, to_apply=%region_21.0 | all-reduce | flops 800 | bytes 6400 | tf_op jit(solution)/shard_map/psum | solution.py:121
  591.3 23.0 fusion.193
  615.4 9.4 fusion.165
  634.1 5.0 fusion.472
  643.4 6.8 convolution_add_fusion.3
  654.3 13.5 fusion.192
  681.7 12.6 collective-permute-done.15
  698.5 25.1 %convert_reduce_fusion.4 = (f32[400]{0:T(512)}, bf16[4,12,32,400]{3,2,1,0:T(8,128)(2,1)S(1)}) fusion(bf16[4,15,38,400]{3,2,1,0:T(8,128)(2,1)S(1)} %get-tuple-element.460, f32[400]{0:T(512)S(1)} %bitcast.605, f32[400]{0:T(512)S(1)} %bitcast.604, f32[400]{0:T(512)S(1)} %bitcast.603, f32[400]{0:T(512)S(1)} %bitcast.602, f32[400]{0:T(512)S(1)} %bitcast.601, ...), kind=kLoop, calls=%fused_computation.567 | loop fusion | flops 104447600 | bytes 55612544 | tf_op jit(solution)/shard_map/reduce_sum | solution.py:270
  730.9 8.3 fusion.429
  739.2 9.3 convert_reduce_fusion.2
  748.5 7.0 fusion.469
  764.0 39.1 %all-reduce.4 = (f32[800]{0:T(1024)S(1)}, f32[800]{0:T(1024)S(1)}) all-reduce(f32[800]{0:T(1024)S(1)} %multiply_reduce_fusion.5, f32[800]{0:T(1024)S(1)} %get-tuple-element.718), channel_id=1, replica_groups=mesh['lat'=4,'lon'=8] {'lat','lon'}, use_global_device_ids=true, to_apply=%region_26.0 | all-reduce | flops 1600 | bytes 12800 | tf_op jit(solution)/shard_map/psum | solution.py:121
  803.7 5.5 fusion.413
  821.0 6.8 reshape.633
  852.5 11.2 reshape.630
  863.7 14.2 reshape.631
  881.5 11.5 convert_reduce_fusion.8
  905.8 5.8 fusion.431
  911.6 10.8 convert_reduce_fusion.1
  945.2 11.9 dynamic-update-slice.4
  957.1 87.2 %dynamic-update-slice.5 = f32[8480000]{0:T(1024)} dynamic-update-slice(f32[8480000]{0:T(1024)} %dynamic-update-slice.4, f32[2560000]{0:T(1024)} %reshape.630, s32[]{} %constant.214) | dynamic-update-slice | bytes 20480004
  1044.3 87.0 %dynamic-update-slice.6 = f32[8480000]{0:T(1024)} dynamic-update-slice(f32[8480000]{0:T(1024)} %dynamic-update-slice.5, f32[2560000]{0:T(1024)} %reshape.631, s32[]{} %constant.215) | dynamic-update-slice | bytes 20480004
  1131.3 17.6 dynamic-update-slice.7
  1148.9 21.8 dynamic-update-slice.8
  1170.6 22.7 dynamic-update-slice.9
  1199.4 554.5 %all-reduce.16 = (bf16[8480000]{0:T(1024)(128)(2,1)}, f32[400]{0:T(512)S(1)}, f32[400]{0:T(512)S(1)}) all-reduce(f32[8480000]{0:T(1024)} %dynamic-update-slice.9, f32[400]{0:T(512)S(1)} %multiply_reduce_fusion.2, f32[400]{0:T(512)S(1)} %get-tuple-element.720), channel_id=3, replica_groups=mesh['lat'=4,'lon'=8] {'lat','lon'}, use_global_device_ids=true, to_apply=%region_187.0.clone | all-reduce | flops 8480800 | bytes 50886400
  1753.9 10.9 fusion.267
  1764.9 8.8 fusion.239
  1773.8 8.3 fusion.266
  1796.0 6.3 broadcast.301
  1802.2 9.0 dynamic-update-slice.1
  1816.5 9.8 collective-permute-done.20
  1832.8 11.5 collective-permute-done.22
  1844.4 16.5 collective-permute-done.23
  1863.4 25.6 %fusion.269 = bf16[4,12,32,400]{3,2,1,0:T(8,128)(2,1)} fusion(f32[4,12,32,400]{3,0,2,1:T(4,128)S(1)} %bitcast.451, bf16[4,12,32,400]{3,2,1,0:T(8,128)(2,1)S(1)} %copy-done.17, bf16[4,12,3,400]{3,2,1,0:T(4,128)(2,1)S(1)} %collective-permute-done.21, bf16[4,12,3,400]{3,2,1,0:T(4,128)(2,1)S(1)} %collective-permute-done.20, ...), kind=kLoop, calls=%fused_computation.563 | loop fusion | flops 102604800 | bytes 56839744 | tf_op jit(solution)/shard_map/convert_element_type | solution.py:293
  1889.0 128.1 %all-reduce.13.cloned.1.call-done = f32[2803200]{0:T(1024)} async-done(((f32[2803200]{0:T(1024)}), f32[2803200]{0:T(1024)}) %all-reduce.13.cloned.1.call-update) | async-done | bytes 11212816
  2017.1 14.6 reshape.640
  2031.7 5.6 reduce_sum.1726
  2042.4 261.0 %all-reduce.15.cloned.1.call-done = bf16[8480000]{0:T(1024)(128)(2,1)} async-done(((bf16[8480000]{0:T(1024)(128)(2,1)}), bf16[8480000]{0:T(1024)(128)(2,1)}) %all-reduce.15.cloned.1.call-update) | async-done | bytes 16960016
  2303.5 10.8 fusion.440
  2314.2 13.5 slice.3016
  2327.7 12.2 copy.216
  2339.9 11.7 slice.3013
  2351.6 6.6 fusion.439
  2365.5 4.7 slice.3026
  (1001 shorter events, 355.8 us)
Async XLA Ops:
  7.2 187.7 %all-gather.20.cloned.1.call-start = ((), (), s32[]{:S(2)}) async-start(), calls=%async_computation.6 | async-start | bytes 1730560 | tf_op jit(solution)/shard_map/all_gather | solution.py:189
  8.0 219.5 %all-gather.12.cloned.1.call-start = ((), (), s32[]{:S(2)}) async-start(), calls=%async_computation | async-start | bytes 2048000 | tf_op jit(solution)/shard_map/all_gather | solution.py:190
  8.7 343.9 %all-gather.14.cloned.1.call-start = ((), (), s32[]{:S(2)}) async-start(), calls=%async_computation.1 | async-start | bytes 6400000 | tf_op jit(solution)/shard_map/all_gather | solution.py:192
  9.4 359.7 %all-gather.16.cloned.1.call-start = ((), (), s32[]{:S(2)}) async-start(), calls=%async_computation.2 | async-start | bytes 7168000 | tf_op jit(solution)/shard_map/all_gather | solution.py:193
  10.0 388.4 %all-gather.22.cloned.1.call-start = ((), (), s32[]{:S(2)}) async-start(), calls=%async_computation.7 | async-start | bytes 1730560 | tf_op jit(solution)/shard_map/all_gather | solution.py:195
  10.6 511.6 %all-gather.18.cloned.1.call-start = ((), (), s32[]{:S(2)}) async-start(), calls=%async_computation.3 | async-start | bytes 2048000 | tf_op jit(solution)/shard_map/all_gather | solution.py:196
  11.6 57.0 %collective-permute-start = (bf16[4,12,3,400]{3,2,1,0:T(4,128)(2,1)}, bf16[4,12,3,400]{3,2,1,0:T(4,128)(2,1)}, u32[]{:S(2)}, u32[]{:S(2)}) collective-permute-start(bf16[4,12,3,400]{3,2,1,0:T(4,128)(2,1)} %get-tuple-element.478), channel_id=1, source_target_pairs={{0,1},{1,2},{2,3},{3,4},{4,5},{5,6},{6,7},{7,0},{8,9},{9,10},{10,1... | collective-permute-start | bytes 345608 | tf_op jit(solution)/shard_map/ppermute | solution.py:17
  12.0 56.6 %collective-permute-start.1 = (bf16[4,12,3,400]{3,2,1,0:T(4,128)(2,1)}, bf16[4,12,3,400]{3,2,1,0:T(4,128)(2,1)}, u32[]{:S(2)}, u32[]{:S(2)}) collective-permute-start(bf16[4,12,3,400]{3,2,1,0:T(4,128)(2,1)} %get-tuple-element.479), channel_id=1, source_target_pairs={{1,0},{2,1},{3,2},{4,3},{5,4},{6,5},{7,6},{0,7},{9,8},{10,9},{11,1... | collective-permute-start | bytes 345608 | tf_op jit(solution)/shard_map/ppermute | solution.py:20
  16.1 2001.0 %all-reduce.13.cloned.1.call-start = ((), (), s32[]{:S(2)}) async-start(), calls=%async_computation.4 | async-start | bytes 22429696
  29.7 45.6 %copy-start.84 = (s32[4,12,32]{2,0,1:T(4,128)S(1)}, s32[4,12,32]{2,0,1:T(4,128)}, u32[]{:S(2)}) copy-start(s32[4,12,32]{2,0,1:T(4,128)} %param.29) | copy-start | bytes 18436
  70.9 47.3 %collective-permute-start.2 = (bf16[4,3,38,400]{3,2,1,0:T(8,128)(2,1)}, bf16[4,3,38,400]{3,2,1,0:T(8,128)(2,1)}, u32[]{:S(2)}, u32[]{:S(2)}) collective-permute-start(bf16[4,3,38,400]{3,2,1,0:T(8,128)(2,1)} %get-tuple-element.469), channel_id=1, source_target_pairs={{0,8},{8,16},{16,24},{1,9},{9,17},{17,25},{2,10},{10,18},{18,26},{... | collective-permute-start | bytes 1094408 | tf_op jit(solution)/shard_map/ppermute | solution.py:17
  73.8 44.4 %collective-permute-start.3 = (bf16[4,3,38,400]{3,2,1,0:T(8,128)(2,1)}, bf16[4,3,38,400]{3,2,1,0:T(8,128)(2,1)}, u32[]{:S(2)}, u32[]{:S(2)}) collective-permute-start(bf16[4,3,38,400]{3,2,1,0:T(8,128)(2,1)} %get-tuple-element.470), channel_id=1, source_target_pairs={{8,0},{16,8},{24,16},{9,1},{17,9},{25,17},{10,2},{18,10},{26,18},{... | collective-permute-start | bytes 1094408 | tf_op jit(solution)/shard_map/ppermute | solution.py:20
  93.9 206.2 %copy-start.73 = (f32[4,6,16]{2,1,0:T(8,128)}, f32[4,6,16]{2,1,0:T(8,128)S(1)}, u32[]{:S(2)}) copy-start(f32[4,6,16]{2,1,0:T(8,128)S(1)} %copy.189) | copy-start | bytes 4612
  250.5 49.6 %copy-start.23 = (bf16[384,800]{1,0:T(8,128)(2,1)}, bf16[384,800]{1,0:T(8,128)(2,1)S(1)}, u32[]{:S(2)}) copy-start(bf16[384,800]{1,0:T(8,128)(2,1)S(1)} %copy.190) | copy-start | bytes 1843204
  250.7 8.0 collective-permute-start.4
  250.8 7.9 collective-permute-start.5
  258.7 41.4 %copy-start.46 = (bf16[4,6,3,800]{3,2,1,0:T(4,128)(2,1)}, bf16[4,6,3,800]{3,2,1,0:T(4,128)(2,1)S(1)}, u32[]{:S(2)}) copy-start(bf16[4,6,3,800]{3,2,1,0:T(4,128)(2,1)S(1)} %collective-permute-done.4) | copy-start | bytes 345604
  258.7 41.4 %copy-start.48 = (bf16[4,6,3,800]{3,2,1,0:T(4,128)(2,1)}, bf16[4,6,3,800]{3,2,1,0:T(4,128)(2,1)S(1)}, u32[]{:S(2)}) copy-start(bf16[4,6,3,800]{3,2,1,0:T(4,128)(2,1)S(1)} %collective-permute-done.5) | copy-start | bytes 345604
  259.4 40.8 %copy-start.101 = (f32[800]{0:T(1024)S(1)}, f32[800]{0:T(1024)}, u32[]{:S(2)}) copy-start(f32[800]{0:T(1024)} %get-tuple-element.367) | copy-start | bytes 9604
  259.4 40.8 %copy-start.102 = (f32[800]{0:T(1024)S(1)}, f32[800]{0:T(1024)}, u32[]{:S(2)}) copy-start(f32[800]{0:T(1024)} %get-tuple-element.368) | copy-start | bytes 9604
  259.4 40.8 %copy-start.103 = (f32[800]{0:T(1024)S(1)}, f32[800]{0:T(1024)}, u32[]{:S(2)}) copy-start(f32[800]{0:T(1024)} %get-tuple-element.369) | copy-start | bytes 9604
  259.4 40.8 %copy-start.104 = (f32[800]{0:T(1024)S(1)}, f32[800]{0:T(1024)}, u32[]{:S(2)}) copy-start(f32[800]{0:T(1024)} %get-tuple-element.370) | copy-start | bytes 9604
  259.4 40.8 %copy-start.105 = (f32[800]{0:T(1024)S(1)}, f32[800]{0:T(1024)}, u32[]{:S(2)}) copy-start(f32[800]{0:T(1024)} %get-tuple-element.371) | copy-start | bytes 9604
  259.4 40.8 %copy-start.106 = (f32[800]{0:T(1024)S(1)}, f32[800]{0:T(1024)}, u32[]{:S(2)}) copy-start(f32[800]{0:T(1024)} %get-tuple-element.372) | copy-start | bytes 9604
  259.4 40.8 %copy-start.107 = (f32[800]{0:T(1024)S(1)}, f32[800]{0:T(1024)}, u32[]{:S(2)}) copy-start(f32[800]{0:T(1024)} %get-tuple-element.373) | copy-start | bytes 9604
  259.4 40.8 %copy-start.108 = (f32[800]{0:T(1024)S(1)}, f32[800]{0:T(1024)}, u32[]{:S(2)}) copy-start(f32[800]{0:T(1024)} %get-tuple-element.374) | copy-start | bytes 9604
  259.5 40.8 %copy-start.109 = (f32[800]{0:T(1024)S(1)}, f32[800]{0:T(1024)}, u32[]{:S(2)}) copy-start(f32[800]{0:T(1024)} %get-tuple-element.375) | copy-start | bytes 9604
  259.5 40.8 %copy-start.110 = (f32[800]{0:T(1024)S(1)}, f32[800]{0:T(1024)}, u32[]{:S(2)}) copy-start(f32[800]{0:T(1024)} %get-tuple-element.376) | copy-start | bytes 9604
  259.5 40.8 %copy-start.111 = (f32[800]{0:T(1024)S(1)}, f32[800]{0:T(1024)}, u32[]{:S(2)}) copy-start(f32[800]{0:T(1024)} %get-tuple-element.377) | copy-start | bytes 9604
  259.5 40.8 %copy-start.112 = (f32[800]{0:T(1024)S(1)}, f32[800]{0:T(1024)}, u32[]{:S(2)}) copy-start(f32[800]{0:T(1024)} %get-tuple-element.378) | copy-start | bytes 9604
  259.8 16.9 collective-permute-start.6
  264.0 34.7 %collective-permute-start.7 = (bf16[4,3,22,800]{3,2,1,0:T(8,128)(2,1)S(1)}, bf16[4,3,22,800]{3,2,1,0:T(8,128)(2,1)S(1)}, u32[]{:S(2)}, u32[]{:S(2)}) collective-permute-start(bf16[4,3,22,800]{3,2,1,0:T(8,128)(2,1)S(1)} %get-tuple-element.487), channel_id=1, source_target_pairs={{8,0},{16,8},{24,16},{9,1},{17,9},{25,17},{10,2},{18,10},{26,18},{... | collective-permute-start | bytes 1267208 | tf_op jit(solution)/shard_map/ppermute | solution.py:20
  300.5 51.9 %copy-start.93 = (f32[800]{0:T(1024)S(1)}, f32[800]{0:T(1024)}, u32[]{:S(2)}) copy-start(f32[800]{0:T(1024)} %convert_element_type.1354) | copy-start | bytes 9604
  300.5 51.9 %copy-start.139 = (f32[800]{0:T(1024)S(1)}, f32[800]{0:T(1024)}, u32[]{:S(2)}) copy-start(f32[800]{0:T(1024)} %convert_element_type.1355) | copy-start | bytes 9604
  312.0 57.1 %copy-start.21 = (f32[4,6,16,800]{3,2,1,0:T(8,128)}, f32[4,6,16,800]{3,2,1,0:T(8,128)S(1)}, u32[]{:S(2)}) copy-start(f32[4,6,16,800]{3,2,1,0:T(8,128)S(1)} %get-tuple-element.445) | copy-start | bytes 3686404
  383.3 8.3 collective-permute-start.8
  383.3 8.3 collective-permute-start.9
  392.2 15.0 collective-permute-start.10
  396.4 23.4 collective-permute-start.11
  398.4 192.9 %copy-start.81 = (f32[4,12,32]{2,1,0:T(8,128)}, f32[4,12,32]{2,1,0:T(8,128)S(1)}, u32[]{:S(2)}) copy-start(f32[4,12,32]{2,1,0:T(8,128)S(1)} %copy.197) | copy-start | bytes 18436
  424.5 63.9 %copy-start.100 = (f32[400]{0:T(512)S(1)}, f32[400]{0:T(512)}, u32[]{:S(2)}) copy-start(f32[400]{0:T(512)} %convert_element_type.1413) | copy-start | bytes 4804
  449.4 42.7 %copy-start.320 = (f32[1600]{0:T(1024)S(1)}, f32[1600]{0:T(1024)}, u32[]{:S(2)}) copy-start(f32[1600]{0:T(1024)} %convert_element_type.1416) | copy-start | bytes 19204
  546.4 44.8 %copy-start.324 = (bf16[400]{0:T(512)(128)(2,1)S(1)}, bf16[400]{0:T(512)(128)(2,1)}, u32[]{:S(2)}) copy-start(bf16[400]{0:T(512)(128)(2,1)} %param.50) | copy-start | bytes 2404
  626.3 41.7 %collective-permute-start.12 = (bf16[4,12,3,400]{3,2,1,0:T(4,128)(2,1)}, bf16[4,12,3,400]{3,2,1,0:T(4,128)(2,1)S(1)}, u32[]{:S(2)}, u32[]{:S(2)}) collective-permute-start(bf16[4,12,3,400]{3,2,1,0:T(4,128)(2,1)} %get-tuple-element.474), channel_id=1, source_target_pairs={{0,1},{1,2},{2,3},{3,4},{4,5},{5,6},{6,7},{7,0},{8,9},{9,10},{10,1... | collective-permute-start | bytes 345608 | tf_op jit(solution)/shard_map/ppermute | solution.py:17
  626.3 41.6 %collective-permute-start.13 = (bf16[4,12,3,400]{3,2,1,0:T(4,128)(2,1)}, bf16[4,12,3,400]{3,2,1,0:T(4,128)(2,1)}, u32[]{:S(2)}, u32[]{:S(2)}) collective-permute-start(bf16[4,12,3,400]{3,2,1,0:T(4,128)(2,1)} %get-tuple-element.475), channel_id=1, source_target_pairs={{1,0},{2,1},{3,2},{4,3},{5,4},{6,5},{7,6},{0,7},{9,8},{10,9},{11,1... | collective-permute-start | bytes 345608 | tf_op jit(solution)/shard_map/ppermute | solution.py:20
  669.9 11.8 collective-permute-start.14
  674.1 20.2 collective-permute-start.15
  759.4 43.7 %copy-start.319 = (bf16[800]{0:T(1024)(128)(2,1)S(1)}, bf16[800]{0:T(1024)(128)(2,1)}, u32[]{:S(2)}) copy-start(bf16[800]{0:T(1024)(128)(2,1)} %param.41) | copy-start | bytes 4804
  759.4 44.3 %copy-start.7 = (bf16[4,9,22,800]{3,2,1,0:T(8,128)(2,1)S(1)}, bf16[4,9,22,800]{3,2,1,0:T(8,128)(2,1)}, u32[]{:S(2)}) copy-start(bf16[4,9,22,800]{3,2,1,0:T(8,128)(2,1)} %copy-done.6) | copy-start | bytes 3801604
  759.4 44.3 %copy-start.87 = (f32[4,6,16]{2,1,0:T(8,128)S(1)}, f32[4,6,16]{2,1,0:T(8,128)}, u32[]{:S(2)}) copy-start(f32[4,6,16]{2,1,0:T(8,128)} %copy.203) | copy-start | bytes 4612
  759.4 44.3 %copy-start.94 = (f32[800]{0:T(1024)S(1)}, f32[800]{0:T(1024)}, u32[]{:S(2)}) copy-start(f32[800]{0:T(1024)} %convert_element_type.1354) | copy-start | bytes 9604
  827.8 9.8 collective-permute-start.16
  827.8 9.8 collective-permute-start.17
  839.2 39.5 %collective-permute-start.18 = (bf16[4,3,22,800]{3,2,1,0:T(8,128)(2,1)}, bf16[4,3,22,800]{3,2,1,0:T(8,128)(2,1)S(1)}, u32[]{:S(2)}, u32[]{:S(2)}) collective-permute-start(bf16[4,3,22,800]{3,2,1,0:T(8,128)(2,1)} %get-tuple-element.482), channel_id=1, source_target_pairs={{0,8},{8,16},{16,24},{1,9},{9,17},{17,25},{2,10},{10,18},{18,26},{... | collective-permute-start | bytes 1267208 | tf_op jit(solution)/shard_map/ppermute | solution.py:17
  843.4 35.3 %collective-permute-start.19 = (bf16[4,3,22,800]{3,2,1,0:T(8,128)(2,1)}, bf16[4,3,22,800]{3,2,1,0:T(8,128)(2,1)}, u32[]{:S(2)}, u32[]{:S(2)}) collective-permute-start(bf16[4,3,22,800]{3,2,1,0:T(8,128)(2,1)} %get-tuple-element.483), channel_id=1, source_target_pairs={{8,0},{16,8},{24,16},{9,1},{17,9},{25,17},{10,2},{18,10},{26,18},{... | collective-permute-start | bytes 1267208 | tf_op jit(solution)/shard_map/ppermute | solution.py:20
  1199.3 554.5 %copy-start.326 = (bf16[400]{0:T(512)(128)(2,1)S(1)}, bf16[400]{0:T(512)(128)(2,1)}, u32[]{:S(2)}) copy-start(bf16[400]{0:T(512)(128)(2,1)} %param.32) | copy-start | bytes 2404
  1199.3 554.6 %copy-start.3 = (bf16[4,15,38,400]{3,2,1,0:T(8,128)(2,1)S(1)}, bf16[4,15,38,400]{3,2,1,0:T(8,128)(2,1)}, u32[]{:S(2)}) copy-start(bf16[4,15,38,400]{3,2,1,0:T(8,128)(2,1)} %copy-done.2) | copy-start | bytes 5472004
  1199.3 554.6 %copy-start.82 = (f32[4,12,32]{2,1,0:T(8,128)S(1)}, f32[4,12,32]{2,1,0:T(8,128)}, u32[]{:S(2)}) copy-start(f32[4,12,32]{2,1,0:T(8,128)} %copy-done.81) | copy-start | bytes 18436
  1199.4 554.6 %copy-start.99 = (f32[400]{0:T(512)S(1)}, f32[400]{0:T(512)}, u32[]{:S(2)}) copy-start(f32[400]{0:T(512)} %convert_element_type.1291) | copy-start | bytes 4804
  1793.6 509.8 %all-reduce.15.cloned.1.call-start = ((), (), s32[]{:S(2)}) async-start(), calls=%async_computation.5 | async-start | bytes 33923072
  1812.9 13.4 collective-permute-start.20
  1813.0 13.3 collective-permute-start.21
  1826.8 17.5 collective-permute-start.22
  1829.4 31.5 %collective-permute-start.23 = (bf16[4,3,38,400]{3,2,1,0:T(8,128)(2,1)S(1)}, bf16[4,3,38,400]{3,2,1,0:T(8,128)(2,1)S(1)}, u32[]{:S(2)}, u32[]{:S(2)}) collective-permute-start(bf16[4,3,38,400]{3,2,1,0:T(8,128)(2,1)S(1)} %get-tuple-element.458), channel_id=1, source_target_pairs={{8,0},{16,8},{24,16},{9,1},{17,9},{25,17},{10,2},{18,10},{26,18},{... | collective-permute-start | bytes 1094408 | tf_op jit(solution)/shard_map/ppermute | solution.py:20
  (309 other events, 4030.3 us)
Sparse Core Ops, SparseCore 0:
  9.9 34.9 all-gather.19
  46.7 43.4 all-gather.11
  92.1 60.4 all-gather.13
  154.3 66.2 all-gather.15
  222.2 29.2 all-gather.21
  253.2 44.0 all-gather.17
  1793.8 223.3 all-reduce.12
  2023.4 280.0 all-reduce.14
